TPU v7x, 128 devices: a whole 4x4x4 slice. The times are simulated.
128 devices in a mesh: dp: 16 (over x, z_hi, core), ctx: 8 (over z_lo, y).
Axes of the slice: x: 4, y: 4, z: 4 (z_hi: 2, z_lo: 2; z = z_hi * 2 + z_lo), core: 2. Of those that a mesh axis runs over, the one named last changes fastest.
Arguments:
- light_flux: float32 [16, 6, 4096], P('dp', None, 'ctx'), may hold values from -6 to 6
- lengths: int32 [16], P('dp'), may hold values from 1024 to 4096, as said below
- offsets: int32 [16, 4096], P('dp', 'ctx'), may hold values from 0 to 3
- start_weight: float32 [512, 3], replicated, may hold values from -3.5 to 3.5
- conv_weight: bfloat16 [2, 1024, 1536], P(None, 'dp'), may hold values from -0.15625 to 0.15625
- gate_bias: float32 [2, 1024], replicated, may hold values from -4 to 4
- mix_first: bfloat16 [1024, 512], P('dp'), may hold values from -0.25 to 0.25
- mix_last: bfloat16 [512, 512], P('dp'), may hold values from -0.25 to 0.25
- end_weight: float32 [6, 512], replicated, may hold values from -0.25 to 0.25
- cotangent: float32 [16, 3, 4096], P('dp', None, 'ctx'), may hold values from -0.0234375 to 0.0234375
Outputs:
- coupled: float32 [16, 3, 4096], P('dp', None, 'ctx')
- grad_start: float32 [512, 3], replicated
- grad_conv: float32 [2, 1024, 1536], P(None, 'dp')
- grad_bias: float32 [2, 1024], replicated
- grad_mix_first: float32 [1024, 512], P('dp')
- grad_mix_last: float32 [512, 512], P('dp')
- grad_end: float32 [6, 512], replicated
Inputs may be any that keep to these rules, and one draw needn't show every extreme that they name: `lengths`: epochs at or past a curve's length are padding; at least one curve has no padding.
All inputs are finite; a program needn't handle non-finite values.
Results may differ from a plain program's by a relative error of at most 0.0091.
Values may be sent and summed in bfloat16 or wider, within the bound.
No kernel may reach another device: no remote copies, remote signals or barrier semaphores. Data moves between devices by JAX's collectives and lax.ppermute only.
A program may use at most 128 MiB of HBM per device.

v0:
```python
import jax
import jax.numpy as jnp
from jax import lax
from jax.sharding import PartitionSpec as P

BUCKETS = 4
highest = lax.Precision.HIGHEST


def from_behind(array, axis, by):
    size = lax.axis_size(axis)
    pairs = [(i, i + by) for i in range(size) if 0 <= i + by < size]
    return lax.ppermute(array, axis, pairs)


def tap_stack(padded, bucket, dilation, reach_len, col_count):
    centre = lax.slice_in_dim(padded, reach_len, reach_len + col_count, axis=1)
    left_tap = lax.slice_in_dim(
        padded, reach_len - dilation, reach_len - dilation + col_count, axis=1
    )
    right_tap = lax.slice_in_dim(
        padded, reach_len + dilation, reach_len + dilation + col_count, axis=1
    )
    for shift_k in range(1, BUCKETS):
        chosen = (bucket == shift_k)[None, :]
        left_start = reach_len - dilation - shift_k
        right_start = reach_len + dilation + shift_k
        left_tap = jnp.where(
            chosen, lax.slice_in_dim(padded, left_start, left_start + col_count, axis=1), left_tap
        )
        right_tap = jnp.where(
            chosen,
            lax.slice_in_dim(padded, right_start, right_start + col_count, axis=1),
            right_tap,
        )
    return jnp.concatenate([left_tap, centre, right_tap], axis=0)


def place_piece(piece, start_col, total_len):
    return jnp.pad(piece, ((0, 0), (start_col, total_len - start_col - piece.shape[1])))


def tap_transpose(d_stacked, bucket, dilation, reach_len, col_count, channels):
    total_len = col_count + 2 * reach_len
    d_left = d_stacked[:channels]
    d_centre = d_stacked[channels : 2 * channels]
    d_right = d_stacked[2 * channels :]
    window = place_piece(d_centre, reach_len, total_len)
    for shift_k in range(BUCKETS):
        chosen = (bucket == shift_k)[None, :]
        left_part = jnp.where(chosen, d_left, 0.0)
        right_part = jnp.where(chosen, d_right, 0.0)
        window = window + place_piece(left_part, reach_len - dilation - shift_k, total_len)
        window = window + place_piece(right_part, reach_len + dilation + shift_k, total_len)
    return window


def gate_forward(preact):
    channels = preact.shape[0] // 2
    return jnp.tanh(preact[:channels]) * jax.nn.sigmoid(preact[channels:])


def gate_backward(preact, d_gated):
    channels = preact.shape[0] // 2
    tangent = jnp.tanh(preact[:channels])
    sigmoid_part = jax.nn.sigmoid(preact[channels:])
    d_upper = d_gated * sigmoid_part * (1.0 - tangent * tangent)
    d_lower = d_gated * tangent * sigmoid_part * (1.0 - sigmoid_part)
    return jnp.concatenate([d_upper, d_lower], axis=0).astype(jnp.bfloat16)


def contract_rows(left_op, right_op, precision=None):
    return lax.dot_general(
        left_op,
        right_op,
        (((1,), (1,)), ((), ())),
        precision=precision,
        preferred_element_type=jnp.float32,
    )


def contract_cols(left_op, right_op, precision=None):
    return lax.dot_general(
        left_op,
        right_op,
        (((0,), (0,)), ((), ())),
        precision=precision,
        preferred_element_type=jnp.float32,
    )


def extend(hidden, reach_len, shard_len):
    pieces_low = []
    pieces_high = []
    remain = reach_len
    distance = 1
    while remain > 0:
        amount = min(shard_len, remain)
        from_low = from_behind(hidden[:, shard_len - amount :], "ctx", distance)
        from_high = from_behind(hidden[:, :amount], "ctx", -distance)
        pieces_low.insert(0, from_low)
        pieces_high.append(from_high)
        remain = remain - amount
        distance = distance + 1
    return jnp.concatenate(pieces_low + [hidden] + pieces_high, axis=1)


def return_rims(grad_window, reach_len, shard_len):
    middle = grad_window[:, reach_len : reach_len + shard_len]
    remain = reach_len
    distance = 1
    end_col = reach_len
    while remain > 0:
        amount = min(shard_len, remain)
        piece_low = grad_window[:, end_col - amount : end_col]
        high_start = reach_len + shard_len + (reach_len - remain)
        piece_high = grad_window[:, high_start : high_start + amount]
        back_low = from_behind(piece_low, "ctx", -distance)
        back_high = from_behind(piece_high, "ctx", distance)
        middle = middle + place_piece(back_low, shard_len - amount, shard_len)
        middle = middle + place_piece(back_high, 0, shard_len)
        end_col = end_col - amount
        remain = remain - amount
        distance = distance + 1
    return middle


def layer_forward(conv_shard, mix_shard, bias_row, stacked):
    full_conv, full_mix = (
        lax.all_gather(conv_shard, "dp", axis=0, tiled=True),
        lax.all_gather(mix_shard, "dp", axis=0, tiled=True),
    )
    preact = jnp.dot(full_conv, stacked, preferred_element_type=jnp.float32) + bias_row[:, None]
    gated = gate_forward(preact).astype(jnp.bfloat16)
    mixed_rows = jnp.dot(full_mix, gated, preferred_element_type=jnp.float32)
    return (preact, gated, mixed_rows, (full_conv, full_mix))


def mix_back(mix_weight, d_mixed):
    return contract_cols(mix_weight, d_mixed)


def conv_back(conv_weight_rows, dz_rows):
    return contract_cols(conv_weight_rows, dz_rows)


def reduce_grad(left_op, right_op):
    full_grad = contract_rows(left_op, right_op)
    summed = lax.psum(full_grad, "ctx")
    return lax.psum_scatter(summed, "dp", scatter_dimension=0, tiled=True)


def local(
    light_flux,
    lengths,
    offsets,
    start_weight,
    conv_weight,
    gate_bias,
    mix_first,
    mix_last,
    end_weight,
    cotangent,
):
    shard_len = light_flux.shape[2]
    half_bands = light_flux.shape[1] // 2
    channels = start_weight.shape[0]
    position = lax.axis_index("ctx") * shard_len + jnp.arange(shard_len, dtype=jnp.int32)
    valid_mask = (position < lengths[0]).astype(jnp.float32)
    bucket = offsets[0]
    first_half = light_flux[0, :half_bands]
    second_half = light_flux[0, half_bands:]
    dilations = (shard_len // 4, shard_len + shard_len // 2)
    reaches = (dilations[0] + BUCKETS - 1, dilations[1] + BUCKETS - 1)
    hidden_first = (jnp.dot(start_weight, first_half, precision=highest) * valid_mask).astype(
        jnp.bfloat16
    )
    stacked_first = tap_stack(
        extend(hidden_first, reaches[0], shard_len), bucket, dilations[0], reaches[0], shard_len
    )
    pre_first, gated_first, mixed_first, kept_first = layer_forward(
        conv_weight[0], mix_first, gate_bias[0], stacked_first
    )
    hidden_second = (
        (hidden_first.astype(jnp.float32) + mixed_first[:channels]) * valid_mask
    ).astype(jnp.bfloat16)
    stacked_second = tap_stack(
        extend(hidden_second, reaches[1], shard_len), bucket, dilations[1], reaches[1], shard_len
    )
    pre_second, gated_second, mixed_second, kept_second = layer_forward(
        conv_weight[1], mix_last, gate_bias[1], stacked_second
    )
    skip_total = mixed_first[channels:] + mixed_second
    end_out = jnp.dot(end_weight, skip_total, precision=highest)
    growth = jnp.exp(end_out[:half_bands])
    coupled = ((growth * second_half + end_out[half_bands:]) * valid_mask)[None]
    d_coupled = cotangent[0] * valid_mask
    d_end = jnp.concatenate([d_coupled * growth * second_half, d_coupled], axis=0)
    grad_end_local = contract_rows(d_end, skip_total, highest)
    d_skip = contract_cols(end_weight, d_end, highest)
    d_skip_b = d_skip.astype(jnp.bfloat16)
    d_gated_second = mix_back(kept_second[1], d_skip_b)
    grad_mix_last = reduce_grad(d_skip_b, gated_second)
    dz_second = gate_backward(pre_second, d_gated_second)
    grad_conv_second = reduce_grad(dz_second, stacked_second)
    bias_second = jnp.sum(dz_second.astype(jnp.float32), axis=1)
    d_stacked_second = conv_back(kept_second[0], dz_second)
    d_window_second = tap_transpose(
        d_stacked_second, bucket, dilations[1], reaches[1], shard_len, channels
    )
    d_field_second = return_rims(d_window_second, reaches[1], shard_len)
    d_mixed_first = jnp.concatenate([d_field_second * valid_mask, d_skip], axis=0).astype(
        jnp.bfloat16
    )
    d_gated_first = mix_back(kept_first[1], d_mixed_first)
    grad_mix_first = reduce_grad(d_mixed_first, gated_first)
    dz_first = gate_backward(pre_first, d_gated_first)
    grad_conv_first = reduce_grad(dz_first, stacked_first)
    bias_first = jnp.sum(dz_first.astype(jnp.float32), axis=1)
    d_stacked_first = conv_back(kept_first[0], dz_first)
    d_window_first = tap_transpose(
        d_stacked_first, bucket, dilations[0], reaches[0], shard_len, channels
    )
    d_hidden_first = d_field_second * valid_mask + return_rims(
        d_window_first, reaches[0], shard_len
    )
    grad_start_local = contract_rows(d_hidden_first * valid_mask, first_half, highest)
    grad_start, grad_bias, grad_end = lax.psum(
        (grad_start_local, jnp.stack([bias_first, bias_second]), grad_end_local), ("dp", "ctx")
    )
    grad_conv = jnp.stack([grad_conv_first, grad_conv_second])
    return (coupled, grad_start, grad_conv, grad_bias, grad_mix_first, grad_mix_last, grad_end)


def solution(mesh):
    in_specs = (
        P("dp", None, "ctx"),
        P("dp"),
        P("dp", "ctx"),
        P(),
        P(None, "dp", None),
        P(),
        P("dp", None),
        P("dp", None),
        P(),
        P("dp", None, "ctx"),
    )
    out_specs = (
        P("dp", None, "ctx"),
        P(),
        P(None, "dp", None),
        P(),
        P("dp", None),
        P("dp", None),
        P(),
    )
    return jax.shard_map(local, mesh=mesh, in_specs=in_specs, out_specs=out_specs, check_vma=False)
```

profile of v0, /device:TPU:1, one launch (start us, length us, event | category | flops | bytes accessed | tf_op | source)
XLA Modules:
  0.0 635.6 jit_solution(13438480193903545730)
XLA Ops:
  7.3 1.8 fusion.83
  12.0 1.7 fusion.11
  13.8 4.0 collective-permute-start
  17.8 1.3 collective-permute-start.1
  20.1 3.8 collective-permute-done.1
  23.9 4.0 fusion.43
  28.0 39.5 %all-gather.8.cloned.1.call-done = bf16[1,1024,1536]{2,1,0:T(8,128)(2,1)} async-done(((bf16[1,64,1536]{2,1,0:T(8,128)(2,1)}), bf16[1,1024,1536]{2,1,0:T(8,128)(2,1)}) %all-gather.8.cloned.1.call-update) | async-done | bytes 3145744 | tf_op jit(solution)/shard_map/all_gather | solution.py:130
  67.5 3.7 add_bitcast_fusion.1
  71.2 1.4 copy-done.10
  73.0 40.6 %all-gather.6.cloned.1.call-done = bf16[1024,512]{1,0:T(8,128)(2,1)} async-done(((bf16[64,512]{1,0:T(8,128)(2,1)}), bf16[1024,512]{1,0:T(8,128)(2,1)}) %all-gather.6.cloned.1.call-update) | async-done | bytes 1048592 | tf_op jit(solution)/shard_map/all_gather | solution.py:131
  113.6 2.0 convolution_bitcast_fusion.2
  115.8 1.3 collective-permute-start.4
  117.1 4.0 collective-permute-start.3
  121.2 4.6 collective-permute-start.2
  125.8 1.3 collective-permute-start.5
  127.1 36.2 %all_gather.15 = bf16[512,512]{1,0:T(8,128)(2,1)} all-gather(bf16[32,512]{1,0:T(8,128)(2,1)S(1)} %copy-done.31), channel_id=1, replica_groups=mesh['dp'=16,'ctx'=8] {'dp'}, dimensions={0}, use_global_device_ids=true | all-gather | bytes 557056 | tf_op jit(solution)/shard_map/all_gather | solution.py:131
  163.4 2.8 fusion.49
  166.2 13.4 %all-gather.10.cloned.1.call-done = bf16[1,1024,1536]{2,1,0:T(8,128)(2,1)} async-done(((bf16[1,64,1536]{2,1,0:T(8,128)(2,1)}), bf16[1,1024,1536]{2,1,0:T(8,128)(2,1)}) %all-gather.10.cloned.1.call-update) | async-done | bytes 3145744 | tf_op jit(solution)/shard_map/all_gather | solution.py:130
  179.6 3.9 add_bitcast_fusion
  188.0 1.3 copy-done.35
  189.3 1.8 convolution_bitcast_fusion.1
  192.0 1.4 pad_add_fusion
  193.4 2.0 copy-done.2
  195.4 1.5 fusion.78
  197.0 1.3 collective-permute-start.6
  198.2 5.0 collective-permute-start.7
  203.2 1.5 fusion.86
  204.8 1.3 fusion.79
  206.1 1.3 collective-permute-start.8
  207.4 5.7 collective-permute-start.9
  213.1 26.5 %collective-permute-done.8 = f32[512,259]{0,1:T(8,128)S(1)} collective-permute-done((f32[512,259]{0,1:T(8,128)S(1)}, f32[512,259]{0,1:T(8,128)S(1)}, u32[]{:S(2)}, u32[]{:S(2)}) %collective-permute-start.8) | collective-permute-done | bytes 530464 | tf_op jit(solution)/shard_map/ppermute | solution.py:13
  239.5 2.9 fusion.76
  243.2 2.1 fusion.31
  245.4 5.7 fusion.32
  252.4 2.8 multiply_convert_fusion.1
  256.2 4.5 fusion.33
  261.9 3.7 convolution_bitcast_fusion
  266.5 1.2 pad_add_fusion.1
  267.7 10.9 %reduce-scatter.11.cloned.1.call-done = f32[32,512]{1,0:T(8,128)} async-done(((f32[512,512]{1,0:T(8,128)}), f32[32,512]{1,0:T(8,128)}) %reduce-scatter.11.cloned.1.call-update) | async-done | bytes 65552 | tf_op jit(solution)/shard_map/reduce_scatter | solution.py:150
  278.6 74.3 %reduce-scatter.9.cloned.1.call-done = f32[64,512]{1,0:T(8,128)} async-done(((f32[1024,512]{1,0:T(8,128)}), f32[64,512]{1,0:T(8,128)}) %reduce-scatter.9.cloned.1.call-update) | async-done | bytes 131088 | tf_op jit(solution)/shard_map/reduce_scatter | solution.py:150
  352.9 93.9 %reduce-scatter.7.cloned.1.call-done = f32[64,1536]{1,0:T(8,128)} async-done(((f32[1024,1536]{1,0:T(8,128)}), f32[64,1536]{1,0:T(8,128)}) %reduce-scatter.7.cloned.1.call-update) | async-done | bytes 393232 | tf_op jit(solution)/shard_map/reduce_scatter | solution.py:150
  446.8 93.0 %reduce-scatter.5.cloned.1.call-done = f32[64,1536]{1,0:T(8,128)} async-done(((f32[1024,1536]{1,0:T(8,128)}), f32[64,1536]{1,0:T(8,128)}) %reduce-scatter.5.cloned.1.call-update) | async-done | bytes 393232 | tf_op jit(solution)/shard_map/reduce_scatter | solution.py:150
  539.9 1.4 collective-permute-start.10
  541.3 4.0 collective-permute-start.11
  549.9 73.7 %all-reduce.22 = (f32[512,3]{0,1:T(4,128)}, f32[2,1024]{1,0:T(2,128)}, f32[6,512]{1,0:T(8,128)}) all-reduce(f32[512,3]{0,1:T(4,128)S(1)} %fusion.15, f32[2,1024]{1,0:T(2,128)S(1)} %pad_maximum_fusion.22, f32[6,512]{1,0:T(8,128)S(1)} %fusion.55), channel_id=1, replica_groups=mesh['dp'=16,'ctx'=8] {'dp','ctx'}, use_global_device_ids=true, to_apply=%region_0.1 | all-reduce | flops 6656 | bytes 53248 | tf_op jit(solution)/shard_map/psum | solution.py:228
  623.7 2.1 pad_maximum_fusion.5
  625.7 1.6 copy.52
  627.3 1.5 copy.53
  (121 shorter events, 19.1 us)
Async XLA Ops:
  7.2 177.9 %copy-start = (f32[6,512]{1,0:T(8,128)S(1)}, f32[6,512]{1,0:T(8,128)}, u32[]{:S(2)}) copy-start(f32[6,512]{1,0:T(8,128)} %param.18) | copy-start | bytes 36868
  7.2 11.9 %copy-start.32 = (f32[2,1024]{1,0:T(2,128)S(1)}, f32[2,1024]{1,0:T(2,128)}, u32[]{:S(2)}) copy-start(f32[2,1024]{1,0:T(2,128)} %param.15) | copy-start | bytes 24580
  7.2 11.9 %copy-start.34 = (s32[1,512]{1,0:T(1,128)S(1)}, s32[1,512]{1,0:T(1,128)}, u32[]{:S(2)}) copy-start(s32[1,512]{1,0:T(1,128)} %param.12) | copy-start | bytes 6148
  7.2 60.3 %all-gather.8.cloned.1.call-start = ((), (), s32[]{:S(2)}) async-start(), calls=%async_computation.5 | async-start | bytes 3342336 | tf_op jit(solution)/shard_map/all_gather | solution.py:130
  9.1 104.5 %all-gather.6.cloned.1.call-start = ((), (), s32[]{:S(2)}) async-start(), calls=%async_computation.4 | async-start | bytes 1114112 | tf_op jit(solution)/shard_map/all_gather | solution.py:131
  9.8 169.8 %all-gather.10.cloned.1.call-start = ((), (), s32[]{:S(2)}) async-start(), calls=%async_computation.6 | async-start | bytes 3342336 | tf_op jit(solution)/shard_map/all_gather | solution.py:130
  10.6 268.1 %reduce-scatter.11.cloned.1.call-start = ((), (), s32[]{:S(2)}) async-start(), calls=%async_computation.10 | async-start | bytes 1114112 | tf_op jit(solution)/shard_map/reduce_scatter | solution.py:150
  13.7 101.8 %copy-start.3 = (bf16[512,512]{0,1:T(8,128)(2,1)}, bf16[512,512]{0,1:T(8,128)(2,1)S(1)}, u32[]{:S(2)}) copy-start(bf16[512,512]{0,1:T(8,128)(2,1)S(1)} %fusion.11) | copy-start | bytes 1572868
  13.8 6.4 collective-permute-start
  17.8 6.1 collective-permute-start.1
  27.9 39.5 %copy-start.26 = (bf16[512,512]{0,1:T(8,128)(2,1)}, bf16[512,512]{0,1:T(8,128)(2,1)S(1)}, u32[]{:S(2)}) copy-start(bf16[512,512]{0,1:T(8,128)(2,1)S(1)} %get-tuple-element.69) | copy-start | bytes 1572868
  28.0 43.2 %copy-start.28 = (bf16[512,512]{0,1:T(8,128)(2,1)}, bf16[512,512]{0,1:T(8,128)(2,1)S(1)}, u32[]{:S(2)}) copy-start(bf16[512,512]{0,1:T(8,128)(2,1)S(1)} %get-tuple-element.70) | copy-start | bytes 1572868
  73.0 40.6 %copy-start.8 = (bf16[512,512]{0,1:T(8,128)(2,1)}, bf16[512,512]{0,1:T(8,128)(2,1)S(1)}, u32[]{:S(2)}) copy-start(bf16[512,512]{0,1:T(8,128)(2,1)S(1)} %multiply_convert_fusion.5) | copy-start | bytes 1572868
  115.6 11.5 %copy-start.31 = (bf16[32,512]{1,0:T(8,128)(2,1)S(1)}, bf16[32,512]{1,0:T(8,128)(2,1)}, u32[]{:S(2)}) copy-start(bf16[32,512]{1,0:T(8,128)(2,1)} %param.17) | copy-start | bytes 98308
  115.8 63.9 %copy-start.6 = (bf16[512,512]{0,1:T(8,128)(2,1)}, bf16[512,512]{0,1:T(8,128)(2,1)S(1)}, u32[]{:S(2)}) copy-start(bf16[512,512]{0,1:T(8,128)(2,1)S(1)} %fusion.25) | copy-start | bytes 1572868
  115.8 47.5 %collective-permute-start.4 = (bf16[512,512]{0,1:T(8,128)(2,1)S(1)}, bf16[512,512]{0,1:T(8,128)(2,1)S(1)}, u32[]{:S(2)}, u32[]{:S(2)}) collective-permute-start(bf16[512,512]{0,1:T(8,128)(2,1)S(1)} %fusion.25), channel_id=1, source_target_pairs={{1,0},{2,1},{3,2},{4,3},{5,4},{6,5},{7,6},{9,8},{10,9},{11,10},{12... | collective-permute-start | bytes 1572872 | tf_op jit(solution)/shard_map/ppermute | solution.py:13
  117.1 46.3 %collective-permute-start.3 = (bf16[512,512]{0,1:T(8,128)(2,1)S(1)}, bf16[512,512]{0,1:T(8,128)(2,1)S(1)}, u32[]{:S(2)}, u32[]{:S(2)}) collective-permute-start(bf16[512,512]{0,1:T(8,128)(2,1)S(1)} %fusion.25), channel_id=1, source_target_pairs={{0,1},{1,2},{2,3},{3,4},{4,5},{5,6},{6,7},{8,9},{9,10},{10,11},{11... | collective-permute-start | bytes 1572872 | tf_op jit(solution)/shard_map/ppermute | solution.py:13
  121.2 42.2 %collective-permute-start.2 = (bf16[512,259]{0,1:T(8,128)(2,1)S(1)}, bf16[512,259]{0,1:T(8,128)(2,1)S(1)}, u32[]{:S(2)}, u32[]{:S(2)}) collective-permute-start(bf16[512,259]{0,1:T(8,128)(2,1)S(1)} %get-tuple-element.71), channel_id=1, source_target_pairs={{0,2},{1,3},{2,4},{3,5},{4,6},{5,7},{8,10},{9,11},{10,12},{11,13},... | collective-permute-start | bytes 795656 | tf_op jit(solution)/shard_map/ppermute | solution.py:13
  125.8 37.6 %collective-permute-start.5 = (bf16[512,259]{0,1:T(8,128)(2,1)S(1)}, bf16[512,259]{0,1:T(8,128)(2,1)S(1)}, u32[]{:S(2)}, u32[]{:S(2)}) collective-permute-start(bf16[512,259]{0,1:T(8,128)(2,1)S(1)} %get-tuple-element.72), channel_id=1, source_target_pairs={{2,0},{3,1},{4,2},{5,3},{6,4},{7,5},{10,8},{11,9},{12,10},{13,11},... | collective-permute-start | bytes 795656 | tf_op jit(solution)/shard_map/ppermute | solution.py:13
  166.2 17.3 %copy-start.13 = (bf16[512,512]{0,1:T(8,128)(2,1)}, bf16[512,512]{0,1:T(8,128)(2,1)S(1)}, u32[]{:S(2)}) copy-start(bf16[512,512]{0,1:T(8,128)(2,1)S(1)} %get-tuple-element.84) | copy-start | bytes 1572868
  184.6 1.5 copy-start.33
  187.1 2.2 copy-start.35
  187.9 3.2 copy-start.16
  187.9 3.2 copy-start.18
  193.4 2.0 copy-start.2
  197.0 42.6 %collective-permute-start.6 = (f32[512,512]{0,1:T(8,128)}, f32[512,512]{0,1:T(8,128)S(1)}, u32[]{:S(2)}, u32[]{:S(2)}) collective-permute-start(f32[512,512]{0,1:T(8,128)} %get-tuple-element.27), channel_id=1, source_target_pairs={{1,0},{2,1},{3,2},{4,3},{5,4},{6,5},{7,6},{9,8},{10,9},{11,10},{12... | collective-permute-start | bytes 3145736 | tf_op jit(solution)/shard_map/ppermute | solution.py:13
  198.2 41.3 %collective-permute-start.7 = (f32[512,512]{0,1:T(8,128)}, f32[512,512]{0,1:T(8,128)}, u32[]{:S(2)}, u32[]{:S(2)}) collective-permute-start(f32[512,512]{0,1:T(8,128)} %get-tuple-element.28), channel_id=1, source_target_pairs={{0,1},{1,2},{2,3},{3,4},{4,5},{5,6},{6,7},{8,9},{9,10},{10,11},{11... | collective-permute-start | bytes 3145736 | tf_op jit(solution)/shard_map/ppermute | solution.py:13
  204.7 148.2 %reduce-scatter.9.cloned.1.call-start = ((), (), s32[]{:S(2)}) async-start(), calls=%async_computation.9 | async-start | bytes 2228224 | tf_op jit(solution)/shard_map/reduce_scatter | solution.py:150
  206.1 33.4 %collective-permute-start.8 = (f32[512,259]{0,1:T(8,128)S(1)}, f32[512,259]{0,1:T(8,128)S(1)}, u32[]{:S(2)}, u32[]{:S(2)}) collective-permute-start(f32[512,259]{0,1:T(8,128)S(1)} %get-tuple-element.29), channel_id=1, source_target_pairs={{2,0},{3,1},{4,2},{5,3},{6,4},{7,5},{10,8},{11,9},{12,10},{13,11},... | collective-permute-start | bytes 1591304 | tf_op jit(solution)/shard_map/ppermute | solution.py:13
  207.4 35.8 %copy-start.9 = (bf16[512,512]{0,1:T(8,128)(2,1)S(1)}, bf16[512,512]{0,1:T(8,128)(2,1)}, u32[]{:S(2)}) copy-start(bf16[512,512]{0,1:T(8,128)(2,1)} %copy-done.8) | copy-start | bytes 1572868
  207.4 32.1 %collective-permute-start.9 = (f32[512,259]{0,1:T(8,128)S(1)}, f32[512,259]{0,1:T(8,128)S(1)}, u32[]{:S(2)}, u32[]{:S(2)}) collective-permute-start(f32[512,259]{0,1:T(8,128)S(1)} %get-tuple-element.30), channel_id=1, source_target_pairs={{0,2},{1,3},{2,4},{3,5},{4,6},{5,7},{8,10},{9,11},{10,12},{11,13},... | collective-permute-start | bytes 1591304 | tf_op jit(solution)/shard_map/ppermute | solution.py:13
  243.2 2.1 copy-start.7
  243.2 2.2 copy-start.14
  243.2 2.2 copy-start.15
  245.3 201.5 %reduce-scatter.7.cloned.1.call-start = ((), (), s32[]{:S(2)}) async-start(), calls=%async_computation.8 | async-start | bytes 6684672 | tf_op jit(solution)/shard_map/reduce_scatter | solution.py:150
  251.1 5.0 copy-start.4
  251.2 288.6 %reduce-scatter.5.cloned.1.call-start = ((), (), s32[]{:S(2)}) async-start(), calls=%async_computation.7 | async-start | bytes 6684672 | tf_op jit(solution)/shard_map/reduce_scatter | solution.py:150
  252.3 3.8 copy-start.27
  252.3 3.8 copy-start.29
  260.8 362.9 %all-reduce.26.cloned.1.call-start = ((), (), s32[]{:S(2)}) async-start(), calls=%async_computation.11 | async-start | bytes 1966080 | tf_op jit(solution)/shard_map/psum | solution.py:149
  267.7 278.9 %copy-start.17 = (bf16[512,512]{0,1:T(8,128)(2,1)S(1)}, bf16[512,512]{0,1:T(8,128)(2,1)}, u32[]{:S(2)}) copy-start(bf16[512,512]{0,1:T(8,128)(2,1)} %copy-done.16) | copy-start | bytes 1572868
  539.8 6.8 %copy-start.19 = (bf16[512,512]{0,1:T(8,128)(2,1)S(1)}, bf16[512,512]{0,1:T(8,128)(2,1)}, u32[]{:S(2)}) copy-start(bf16[512,512]{0,1:T(8,128)(2,1)} %copy-done.18) | copy-start | bytes 1572868
  539.8 6.9 %copy-start.22 = (bf16[512,512]{0,1:T(8,128)(2,1)S(1)}, bf16[512,512]{0,1:T(8,128)(2,1)}, u32[]{:S(2)}) copy-start(bf16[512,512]{0,1:T(8,128)(2,1)} %copy-done.20) | copy-start | bytes 1572868
  539.8 6.9 %copy-start.25 = (bf16[512,512]{0,1:T(8,128)(2,1)S(1)}, bf16[512,512]{0,1:T(8,128)(2,1)}, u32[]{:S(2)}) copy-start(bf16[512,512]{0,1:T(8,128)(2,1)} %copy-done.23) | copy-start | bytes 1572868
  539.9 9.2 %copy-start.5 = (f32[512,512]{0,1:T(8,128)S(1)}, f32[512,512]{0,1:T(8,128)}, u32[]{:S(2)}) copy-start(f32[512,512]{0,1:T(8,128)} %get-tuple-element.26) | copy-start | bytes 3145732
  539.9 8.3 %collective-permute-start.10 = (f32[512,131]{0,1:T(8,128)S(1)}, f32[512,131]{0,1:T(8,128)S(1)}, u32[]{:S(2)}, u32[]{:S(2)}) collective-permute-start(f32[512,131]{0,1:T(8,128)S(1)} %get-tuple-element.67), channel_id=1, source_target_pairs={{1,0},{2,1},{3,2},{4,3},{5,4},{6,5},{7,6},{9,8},{10,9},{11,10},{12... | collective-permute-start | bytes 804872 | tf_op jit(solution)/shard_map/ppermute | solution.py:13
  541.3 7.7 %collective-permute-start.11 = (f32[512,131]{0,1:T(8,128)S(1)}, f32[512,131]{0,1:T(8,128)S(1)}, u32[]{:S(2)}, u32[]{:S(2)}) collective-permute-start(f32[512,131]{0,1:T(8,128)S(1)} %get-tuple-element.68), channel_id=1, source_target_pairs={{0,1},{1,2},{2,3},{3,4},{4,5},{5,6},{6,7},{8,9},{9,10},{10,11},{11... | collective-permute-start | bytes 804872 | tf_op jit(solution)/shard_map/ppermute | solution.py:13
  549.1 79.7 %copy-start.1 = (f32[6,512]{1,0:T(8,128)S(1)}, f32[6,512]{1,0:T(8,128)}, u32[]{:S(2)}) copy-start(f32[6,512]{1,0:T(8,128)} %param.18) | copy-start | bytes 36868
  (8 other events, 8.5 us)
Sparse Core Ops, SparseCore 0:
  11.0 56.4 all-gather.7
  69.9 43.6 all-gather.5
  116.0 63.5 all-gather.9
  204.8 73.7 reduce-scatter.10
  282.9 69.9 reduce-scatter.8
  357.5 89.2 reduce-scatter.6
  451.5 88.2 reduce-scatter.4
  542.8 71.9 all-reduce.25
where the time goes:
time: 637 us; the launch traced here: 636 us
  waiting for transfers between devices  400 us (63%)
  blocking collectives  110 us (17%)
  matrix products  38.1 us (6%)
  starting transfers between devices  35.7 us (6%)
  local copies, waits for them, and re-layouts  18.5 us (3%)
  other arithmetic  17.6 us (3%)
  between operations  15.4 us (2%)
    reduce_scatter x4, waiting for transfers between devices, reduce_grad(): return lax.psum_scatter(summed, 'dp', scatter_dimension=0, tiled=True)  272 us
    psum x1, blocking collectives, local(): lax.psum((grad_start_local, jnp.stack([bias_first, bias_second]), grad_en...  73.7 us
    all_gather x2, waiting for transfers between devices, layer_forward(): lax.all_gather(conv_shard, 'dp', axis=0, tiled=True)  52.9 us
    all_gather x1, waiting for transfers between devices, layer_forward(): lax.all_gather(mix_shard, 'dp', axis=0, tiled=True)  40.6 us
    all_gather x1, blocking collectives, layer_forward(): lax.all_gather(mix_shard, 'dp', axis=0, tiled=True)  36.2 us
    ppermute x12, starting transfers between devices, from_behind(): return lax.ppermute(array, axis, pairs)  35.2 us
    ppermute x12, waiting for transfers between devices, from_behind(): return lax.ppermute(array, axis, pairs)  33.3 us
    dot_general x6, matrix products, contract_rows(): lax.dot_general(left_op, right_op, (((1,), (1,)), ((), ())), precision=pr...  15.2 us
  transfers between devices with their start and end apart: 20, of which 12 were waited for; matrix products, arithmetic and copies ran while one was open for 7% of the time, Pallas kernels for 0%

commit v1 on v0

--- a/solution.py
+++ b/solution.py
@@ -225,8 +225,13 @@
         d_window_first, reaches[0], shard_len
     )
     grad_start_local = contract_rows(d_hidden_first * valid_mask, first_half, highest)
-    grad_start, grad_bias, grad_end = lax.psum(
-        (grad_start_local, jnp.stack([bias_first, bias_second]), grad_end_local), ("dp", "ctx")
+
+    def update_cards_on(content, which_axis, ax_name):
+        w_next = lax.psum(lax.psum(content, which_axis), ax_name)
+        return w_next
+
+    grad_start, grad_bias, grad_end = update_cards_on(
+        (grad_start_local, jnp.stack([bias_first, bias_second]), grad_end_local), "dp", "ctx"
     )
     grad_conv = jnp.stack([grad_conv_first, grad_conv_second])
     return (coupled, grad_start, grad_conv, grad_bias, grad_mix_first, grad_mix_last, grad_end)

time: 637 us -> 668 us (1.049)
  the two profiles are of different devices: /device:TPU:1 before, /device:TPU:32 now
where the time goes in v1:
time: 668 us; the launch traced here: 667 us
  waiting for transfers between devices  411 us (62%)
  blocking collectives  120 us (18%)
  starting transfers between devices  46.5 us (7%)
  matrix products  38.1 us (6%)
  local copies, waits for them, and re-layouts  18.5 us (3%)
  other arithmetic  17.5 us (3%)
  between operations  15.4 us (2%)
    reduce_scatter x4, waiting for transfers between devices, reduce_grad(): return lax.psum_scatter(summed, 'dp', scatter_dimension=0, tiled=True)  258 us
    psum x2, blocking collectives, update_cards_on(): w_next = lax.psum(lax.psum(content, which_axis), ax_name)  96.4 us
    all_gather x2, waiting for transfers between devices, layer_forward(): lax.all_gather(conv_shard, 'dp', axis=0, tiled=True)  58.2 us
    ppermute x12, waiting for transfers between devices, from_behind(): return lax.ppermute(array, axis, pairs)  53 us
    ppermute x12, starting transfers between devices, from_behind(): return lax.ppermute(array, axis, pairs)  46 us
    all_gather x1, waiting for transfers between devices, layer_forward(): lax.all_gather(mix_shard, 'dp', axis=0, tiled=True)  40.6 us
    all_gather x1, blocking collectives, layer_forward(): lax.all_gather(mix_shard, 'dp', axis=0, tiled=True)  23.5 us
    dot_general x6, matrix products, contract_rows(): lax.dot_general(left_op, right_op, (((1,), (1,)), ((), ())), precision=pr...  15.2 us
  transfers between devices with their start and end apart: 20, of which 13 were waited for; matrix products, arithmetic and copies ran while one was open for 7% of the time, Pallas kernels for 0%

profile of v1, /device:TPU:32, one launch (start us, length us, event | category | flops | bytes accessed | tf_op | source)
XLA Modules:
  0.0 667.4 jit_solution(110341091393774015)
XLA Ops:
  7.3 1.8 fusion.83
  12.0 1.7 fusion.11
  13.8 3.5 collective-permute-start
  17.2 4.5 collective-permute-start.1
  21.8 1.4 collective-permute-done
  24.3 4.0 fusion.43
  28.4 36.6 %all-gather.8.cloned.1.call-done = bf16[1,1024,1536]{2,1,0:T(8,128)(2,1)} async-done(((bf16[1,64,1536]{2,1,0:T(8,128)(2,1)}), bf16[1,1024,1536]{2,1,0:T(8,128)(2,1)}) %all-gather.8.cloned.1.call-update) | async-done | bytes 3145744 | tf_op jit(solution)/shard_map/all_gather | solution.py:130
  65.0 3.7 add_bitcast_fusion.1
  68.7 1.4 copy-done.10
  70.5 40.6 %all-gather.6.cloned.1.call-done = bf16[1024,512]{1,0:T(8,128)(2,1)} async-done(((bf16[64,512]{1,0:T(8,128)(2,1)}), bf16[1024,512]{1,0:T(8,128)(2,1)}) %all-gather.6.cloned.1.call-update) | async-done | bytes 1048592 | tf_op jit(solution)/shard_map/all_gather | solution.py:131
  111.1 2.0 convolution_bitcast_fusion.2
  113.2 5.5 collective-permute-start.4
  118.7 1.9 collective-permute-start.3
  120.7 3.4 collective-permute-start.2
  124.1 4.8 collective-permute-start.5
  129.0 23.5 %all_gather.15 = bf16[512,512]{1,0:T(8,128)(2,1)} all-gather(bf16[32,512]{1,0:T(8,128)(2,1)S(1)} %copy-done.31), channel_id=1, replica_groups=mesh['dp'=16,'ctx'=8] {'dp'}, dimensions={0}, use_global_device_ids=true | all-gather | bytes 557056 | tf_op jit(solution)/shard_map/all_gather | solution.py:131
  152.6 2.8 fusion.49
  155.4 21.7 %all-gather.10.cloned.1.call-done = bf16[1,1024,1536]{2,1,0:T(8,128)(2,1)} async-done(((bf16[1,64,1536]{2,1,0:T(8,128)(2,1)}), bf16[1,1024,1536]{2,1,0:T(8,128)(2,1)}) %all-gather.10.cloned.1.call-update) | async-done | bytes 3145744 | tf_op jit(solution)/shard_map/all_gather | solution.py:130
  177.1 3.9 add_bitcast_fusion
  186.8 1.8 convolution_bitcast_fusion.1
  189.5 1.4 pad_add_fusion
  190.9 2.0 copy-done.2
  192.9 1.5 fusion.78
  194.4 5.4 collective-permute-start.6
  199.9 1.9 collective-permute-start.7
  201.8 1.4 fusion.86
  204.6 4.2 collective-permute-start.8
  208.8 3.3 collective-permute-start.9
  212.2 26.0 %collective-permute-done.8 = f32[512,259]{0,1:T(8,128)S(1)} collective-permute-done((f32[512,259]{0,1:T(8,128)S(1)}, f32[512,259]{0,1:T(8,128)S(1)}, u32[]{:S(2)}, u32[]{:S(2)}) %collective-permute-start.8) | collective-permute-done | bytes 530464 | tf_op jit(solution)/shard_map/ppermute | solution.py:13
  238.1 12.4 %collective-permute-done.9 = f32[512,259]{0,1:T(8,128)S(1)} collective-permute-done((f32[512,259]{0,1:T(8,128)S(1)}, f32[512,259]{0,1:T(8,128)S(1)}, u32[]{:S(2)}, u32[]{:S(2)}) %collective-permute-start.9) | collective-permute-done | bytes 530464 | tf_op jit(solution)/shard_map/ppermute | solution.py:13
  250.6 1.8 collective-permute-done.7
  252.4 2.9 fusion.76
  256.1 2.1 fusion.31
  258.3 5.7 fusion.32
  265.2 2.9 multiply_convert_fusion.1
  269.1 4.5 fusion.33
  274.8 3.7 convolution_bitcast_fusion
  280.7 72.1 %reduce-scatter.9.cloned.1.call-done = f32[64,512]{1,0:T(8,128)} async-done(((f32[1024,512]{1,0:T(8,128)}), f32[64,512]{1,0:T(8,128)}) %reduce-scatter.9.cloned.1.call-update) | async-done | bytes 131088 | tf_op jit(solution)/shard_map/reduce_scatter | solution.py:150
  352.8 93.1 %reduce-scatter.7.cloned.1.call-done = f32[64,1536]{1,0:T(8,128)} async-done(((f32[1024,1536]{1,0:T(8,128)}), f32[64,1536]{1,0:T(8,128)}) %reduce-scatter.7.cloned.1.call-update) | async-done | bytes 393232 | tf_op jit(solution)/shard_map/reduce_scatter | solution.py:150
  445.9 92.9 %reduce-scatter.5.cloned.1.call-done = f32[64,1536]{1,0:T(8,128)} async-done(((f32[1024,1536]{1,0:T(8,128)}), f32[64,1536]{1,0:T(8,128)}) %reduce-scatter.5.cloned.1.call-update) | async-done | bytes 393232 | tf_op jit(solution)/shard_map/reduce_scatter | solution.py:150
  538.9 5.6 collective-permute-start.10
  544.5 1.9 collective-permute-start.11
  549.2 9.1 %collective-permute-done.11 = f32[512,131]{0,1:T(8,128)S(1)} collective-permute-done((f32[512,131]{0,1:T(8,128)S(1)}, f32[512,131]{0,1:T(8,128)S(1)}, u32[]{:S(2)}, u32[]{:S(2)}) %collective-permute-start.11) | collective-permute-done | bytes 268320 | tf_op jit(solution)/shard_map/ppermute | solution.py:13
  559.1 65.1 %all-reduce.22 = (f32[512,3]{0,1:T(4,128)S(1)}, f32[2,1024]{1,0:T(2,128)S(1)}, f32[6,512]{1,0:T(8,128)S(1)}) all-reduce(f32[512,3]{0,1:T(4,128)S(1)} %fusion.15, f32[2,1024]{1,0:T(2,128)S(1)} %pad_maximum_fusion.22, f32[6,512]{1,0:T(8,128)S(1)} %fusion.55), channel_id=1, replica_groups=mesh['dp'=16,'ctx'=8] {'dp'}, use_global_device_ids=true, to_apply=%region_0.1 | all-reduce | flops 6656 | bytes 53248 | tf_op jit(solution)/shard_map/psum | solution.py:230
  624.2 31.3 %all-reduce.23 = (f32[512,3]{0,1:T(4,128)}, f32[2,1024]{1,0:T(2,128)}, f32[6,512]{1,0:T(8,128)}) all-reduce(f32[512,3]{0,1:T(4,128)S(1)} %get-tuple-element.18, f32[2,1024]{1,0:T(2,128)S(1)} %get-tuple-element.19, f32[6,512]{1,0:T(8,128)S(1)} %get-tuple-element.20), channel_id=1, replica_groups=mesh['dp'=16,'ctx'=8] {'ctx'}, use_global_device_ids=true, to_apply=%region_1.2 | all-reduce | flops 6656 | bytes 53248 | tf_op jit(solution)/shard_map/psum | solution.py:230
  655.5 2.0 pad_maximum_fusion.5
  657.5 1.6 copy.52
  659.1 1.5 copy.53
  (122 shorter events, 22.2 us)
Async XLA Ops:
  7.2 175.3 %copy-start = (f32[6,512]{1,0:T(8,128)S(1)}, f32[6,512]{1,0:T(8,128)}, u32[]{:S(2)}) copy-start(f32[6,512]{1,0:T(8,128)} %param.18) | copy-start | bytes 36868
  7.2 14.5 %copy-start.32 = (f32[2,1024]{1,0:T(2,128)S(1)}, f32[2,1024]{1,0:T(2,128)}, u32[]{:S(2)}) copy-start(f32[2,1024]{1,0:T(2,128)} %param.15) | copy-start | bytes 24580
  7.2 14.6 %copy-start.34 = (s32[1,512]{1,0:T(1,128)S(1)}, s32[1,512]{1,0:T(1,128)}, u32[]{:S(2)}) copy-start(s32[1,512]{1,0:T(1,128)} %param.12) | copy-start | bytes 6148
  7.2 57.8 %all-gather.8.cloned.1.call-start = ((), (), s32[]{:S(2)}) async-start(), calls=%async_computation.5 | async-start | bytes 3342336 | tf_op jit(solution)/shard_map/all_gather | solution.py:130
  9.1 102.0 %all-gather.6.cloned.1.call-start = ((), (), s32[]{:S(2)}) async-start(), calls=%async_computation.4 | async-start | bytes 1114112 | tf_op jit(solution)/shard_map/all_gather | solution.py:131
  9.8 167.3 %all-gather.10.cloned.1.call-start = ((), (), s32[]{:S(2)}) async-start(), calls=%async_computation.6 | async-start | bytes 3342336 | tf_op jit(solution)/shard_map/all_gather | solution.py:130
  10.5 270.1 %reduce-scatter.11.cloned.1.call-start = ((), (), s32[]{:S(2)}) async-start(), calls=%async_computation.10 | async-start | bytes 1114112 | tf_op jit(solution)/shard_map/reduce_scatter | solution.py:150
  13.7 99.3 %copy-start.3 = (bf16[512,512]{0,1:T(8,128)(2,1)}, bf16[512,512]{0,1:T(8,128)(2,1)S(1)}, u32[]{:S(2)}) copy-start(bf16[512,512]{0,1:T(8,128)(2,1)S(1)} %fusion.11) | copy-start | bytes 1572868
  13.8 9.4 %collective-permute-start = (bf16[512,131]{0,1:T(8,128)(2,1)S(1)}, bf16[512,131]{0,1:T(8,128)(2,1)S(1)}, u32[]{:S(2)}, u32[]{:S(2)}) collective-permute-start(bf16[512,131]{0,1:T(8,128)(2,1)S(1)} %get-tuple-element.76), channel_id=1, source_target_pairs={{0,1},{1,2},{2,3},{3,4},{4,5},{5,6},{6,7},{8,9},{9,10},{10,11},{11... | collective-permute-start | bytes 402440 | tf_op jit(solution)/shard_map/ppermute | solution.py:13
  17.2 7.1 %collective-permute-start.1 = (bf16[512,131]{0,1:T(8,128)(2,1)S(1)}, bf16[512,131]{0,1:T(8,128)(2,1)S(1)}, u32[]{:S(2)}, u32[]{:S(2)}) collective-permute-start(bf16[512,131]{0,1:T(8,128)(2,1)S(1)} %get-tuple-element.77), channel_id=1, source_target_pairs={{1,0},{2,1},{3,2},{4,3},{5,4},{6,5},{7,6},{9,8},{10,9},{11,10},{12... | collective-permute-start | bytes 402440 | tf_op jit(solution)/shard_map/ppermute | solution.py:13
  28.4 36.6 %copy-start.26 = (bf16[512,512]{0,1:T(8,128)(2,1)}, bf16[512,512]{0,1:T(8,128)(2,1)S(1)}, u32[]{:S(2)}) copy-start(bf16[512,512]{0,1:T(8,128)(2,1)S(1)} %get-tuple-element.72) | copy-start | bytes 1572868
  28.4 40.3 %copy-start.28 = (bf16[512,512]{0,1:T(8,128)(2,1)}, bf16[512,512]{0,1:T(8,128)(2,1)S(1)}, u32[]{:S(2)}) copy-start(bf16[512,512]{0,1:T(8,128)(2,1)S(1)} %get-tuple-element.73) | copy-start | bytes 1572868
  70.5 40.6 %copy-start.8 = (bf16[512,512]{0,1:T(8,128)(2,1)}, bf16[512,512]{0,1:T(8,128)(2,1)S(1)}, u32[]{:S(2)}) copy-start(bf16[512,512]{0,1:T(8,128)(2,1)S(1)} %multiply_convert_fusion.5) | copy-start | bytes 1572868
  113.0 15.9 %copy-start.31 = (bf16[32,512]{1,0:T(8,128)(2,1)S(1)}, bf16[32,512]{1,0:T(8,128)(2,1)}, u32[]{:S(2)}) copy-start(bf16[32,512]{1,0:T(8,128)(2,1)} %param.17) | copy-start | bytes 98308
  113.2 63.9 %copy-start.6 = (bf16[512,512]{0,1:T(8,128)(2,1)}, bf16[512,512]{0,1:T(8,128)(2,1)S(1)}, u32[]{:S(2)}) copy-start(bf16[512,512]{0,1:T(8,128)(2,1)S(1)} %fusion.25) | copy-start | bytes 1572868
  113.2 39.3 %collective-permute-start.4 = (bf16[512,512]{0,1:T(8,128)(2,1)S(1)}, bf16[512,512]{0,1:T(8,128)(2,1)S(1)}, u32[]{:S(2)}, u32[]{:S(2)}) collective-permute-start(bf16[512,512]{0,1:T(8,128)(2,1)S(1)} %fusion.25), channel_id=1, source_target_pairs={{1,0},{2,1},{3,2},{4,3},{5,4},{6,5},{7,6},{9,8},{10,9},{11,10},{12... | collective-permute-start | bytes 1572872 | tf_op jit(solution)/shard_map/ppermute | solution.py:13
  118.7 33.9 %collective-permute-start.3 = (bf16[512,512]{0,1:T(8,128)(2,1)S(1)}, bf16[512,512]{0,1:T(8,128)(2,1)S(1)}, u32[]{:S(2)}, u32[]{:S(2)}) collective-permute-start(bf16[512,512]{0,1:T(8,128)(2,1)S(1)} %fusion.25), channel_id=1, source_target_pairs={{0,1},{1,2},{2,3},{3,4},{4,5},{5,6},{6,7},{8,9},{9,10},{10,11},{11... | collective-permute-start | bytes 1572872 | tf_op jit(solution)/shard_map/ppermute | solution.py:13
  120.7 31.9 %collective-permute-start.2 = (bf16[512,259]{0,1:T(8,128)(2,1)S(1)}, bf16[512,259]{0,1:T(8,128)(2,1)S(1)}, u32[]{:S(2)}, u32[]{:S(2)}) collective-permute-start(bf16[512,259]{0,1:T(8,128)(2,1)S(1)} %get-tuple-element.74), channel_id=1, source_target_pairs={{0,2},{1,3},{2,4},{3,5},{4,6},{5,7},{8,10},{9,11},{10,12},{11,13},... | collective-permute-start | bytes 795656 | tf_op jit(solution)/shard_map/ppermute | solution.py:13
  124.1 28.4 %collective-permute-start.5 = (bf16[512,259]{0,1:T(8,128)(2,1)S(1)}, bf16[512,259]{0,1:T(8,128)(2,1)S(1)}, u32[]{:S(2)}, u32[]{:S(2)}) collective-permute-start(bf16[512,259]{0,1:T(8,128)(2,1)S(1)} %get-tuple-element.75), channel_id=1, source_target_pairs={{2,0},{3,1},{4,2},{5,3},{6,4},{7,5},{10,8},{11,9},{12,10},{13,11},... | collective-permute-start | bytes 795656 | tf_op jit(solution)/shard_map/ppermute | solution.py:13
  155.4 25.6 %copy-start.13 = (bf16[512,512]{0,1:T(8,128)(2,1)}, bf16[512,512]{0,1:T(8,128)(2,1)S(1)}, u32[]{:S(2)}) copy-start(bf16[512,512]{0,1:T(8,128)(2,1)S(1)} %get-tuple-element.87) | copy-start | bytes 1572868
  182.0 1.5 copy-start.33
  184.6 2.2 copy-start.35
  185.4 3.2 copy-start.16
  185.4 3.2 copy-start.18
  190.9 2.0 copy-start.2
  194.4 56.1 %collective-permute-start.6 = (f32[512,512]{0,1:T(8,128)}, f32[512,512]{0,1:T(8,128)S(1)}, u32[]{:S(2)}, u32[]{:S(2)}) collective-permute-start(f32[512,512]{0,1:T(8,128)} %get-tuple-element.30), channel_id=1, source_target_pairs={{1,0},{2,1},{3,2},{4,3},{5,4},{6,5},{7,6},{9,8},{10,9},{11,10},{12... | collective-permute-start | bytes 3145736 | tf_op jit(solution)/shard_map/ppermute | solution.py:13
  199.9 52.5 %collective-permute-start.7 = (f32[512,512]{0,1:T(8,128)}, f32[512,512]{0,1:T(8,128)}, u32[]{:S(2)}, u32[]{:S(2)}) collective-permute-start(f32[512,512]{0,1:T(8,128)} %get-tuple-element.31), channel_id=1, source_target_pairs={{0,1},{1,2},{2,3},{3,4},{4,5},{5,6},{6,7},{8,9},{9,10},{10,11},{11... | collective-permute-start | bytes 3145736 | tf_op jit(solution)/shard_map/ppermute | solution.py:13
  203.3 149.5 %reduce-scatter.9.cloned.1.call-start = ((), (), s32[]{:S(2)}) async-start(), calls=%async_computation.9 | async-start | bytes 2228224 | tf_op jit(solution)/shard_map/reduce_scatter | solution.py:150
  204.6 33.5 %collective-permute-start.8 = (f32[512,259]{0,1:T(8,128)S(1)}, f32[512,259]{0,1:T(8,128)S(1)}, u32[]{:S(2)}, u32[]{:S(2)}) collective-permute-start(f32[512,259]{0,1:T(8,128)S(1)} %get-tuple-element.32), channel_id=1, source_target_pairs={{2,0},{3,1},{4,2},{5,3},{6,4},{7,5},{10,8},{11,9},{12,10},{13,11},... | collective-permute-start | bytes 1591304 | tf_op jit(solution)/shard_map/ppermute | solution.py:13
  208.8 47.3 %copy-start.9 = (bf16[512,512]{0,1:T(8,128)(2,1)S(1)}, bf16[512,512]{0,1:T(8,128)(2,1)}, u32[]{:S(2)}) copy-start(bf16[512,512]{0,1:T(8,128)(2,1)} %copy-done.8) | copy-start | bytes 1572868
  208.8 41.7 %collective-permute-start.9 = (f32[512,259]{0,1:T(8,128)S(1)}, f32[512,259]{0,1:T(8,128)S(1)}, u32[]{:S(2)}, u32[]{:S(2)}) collective-permute-start(f32[512,259]{0,1:T(8,128)S(1)} %get-tuple-element.33), channel_id=1, source_target_pairs={{0,2},{1,3},{2,4},{3,5},{4,6},{5,7},{8,10},{9,11},{10,12},{11,13},... | collective-permute-start | bytes 1591304 | tf_op jit(solution)/shard_map/ppermute | solution.py:13
  256.1 2.2 copy-start.7
  256.1 2.2 copy-start.14
  256.1 2.2 copy-start.15
  258.2 187.7 %reduce-scatter.7.cloned.1.call-start = ((), (), s32[]{:S(2)}) async-start(), calls=%async_computation.8 | async-start | bytes 6684672 | tf_op jit(solution)/shard_map/reduce_scatter | solution.py:150
  264.0 5.1 copy-start.4
  264.0 274.8 %reduce-scatter.5.cloned.1.call-start = ((), (), s32[]{:S(2)}) async-start(), calls=%async_computation.7 | async-start | bytes 6684672 | tf_op jit(solution)/shard_map/reduce_scatter | solution.py:150
  265.2 3.9 copy-start.27
  265.2 3.9 copy-start.29
  273.7 381.8 %all-reduce.27.cloned.1.call-start = ((), (), s32[]{:S(2)}) async-start(), calls=%async_computation.11 | async-start | bytes 1966080 | tf_op jit(solution)/shard_map/psum | solution.py:149
  280.6 267.1 %copy-start.17 = (bf16[512,512]{0,1:T(8,128)(2,1)S(1)}, bf16[512,512]{0,1:T(8,128)(2,1)}, u32[]{:S(2)}) copy-start(bf16[512,512]{0,1:T(8,128)(2,1)} %copy-done.16) | copy-start | bytes 1572868
  538.8 8.9 %copy-start.19 = (bf16[512,512]{0,1:T(8,128)(2,1)S(1)}, bf16[512,512]{0,1:T(8,128)(2,1)}, u32[]{:S(2)}) copy-start(bf16[512,512]{0,1:T(8,128)(2,1)} %copy-done.18) | copy-start | bytes 1572868
  538.9 9.0 %copy-start.22 = (bf16[512,512]{0,1:T(8,128)(2,1)S(1)}, bf16[512,512]{0,1:T(8,128)(2,1)}, u32[]{:S(2)}) copy-start(bf16[512,512]{0,1:T(8,128)(2,1)} %copy-done.20) | copy-start | bytes 1572868
  538.9 9.0 %copy-start.25 = (bf16[512,512]{0,1:T(8,128)(2,1)S(1)}, bf16[512,512]{0,1:T(8,128)(2,1)}, u32[]{:S(2)}) copy-start(bf16[512,512]{0,1:T(8,128)(2,1)} %copy-done.23) | copy-start | bytes 1572868
  538.9 19.4 %copy-start.5 = (f32[512,512]{0,1:T(8,128)S(1)}, f32[512,512]{0,1:T(8,128)}, u32[]{:S(2)}) copy-start(f32[512,512]{0,1:T(8,128)} %get-tuple-element.29) | copy-start | bytes 3145732
  538.9 10.2 %collective-permute-start.10 = (f32[512,131]{0,1:T(8,128)S(1)}, f32[512,131]{0,1:T(8,128)S(1)}, u32[]{:S(2)}, u32[]{:S(2)}) collective-permute-start(f32[512,131]{0,1:T(8,128)S(1)} %get-tuple-element.70), channel_id=1, source_target_pairs={{1,0},{2,1},{3,2},{4,3},{5,4},{6,5},{7,6},{9,8},{10,9},{11,10},{12... | collective-permute-start | bytes 804872 | tf_op jit(solution)/shard_map/ppermute | solution.py:13
  544.5 13.7 %collective-permute-start.11 = (f32[512,131]{0,1:T(8,128)S(1)}, f32[512,131]{0,1:T(8,128)S(1)}, u32[]{:S(2)}, u32[]{:S(2)}) collective-permute-start(f32[512,131]{0,1:T(8,128)S(1)} %get-tuple-element.71), channel_id=1, source_target_pairs={{0,1},{1,2},{2,3},{3,4},{4,5},{5,6},{6,7},{8,9},{9,10},{10,11},{11... | collective-permute-start | bytes 804872 | tf_op jit(solution)/shard_map/ppermute | solution.py:13
  558.3 102.3 %copy-start.1 = (f32[6,512]{1,0:T(8,128)S(1)}, f32[6,512]{1,0:T(8,128)}, u32[]{:S(2)}) copy-start(f32[6,512]{1,0:T(8,128)} %param.18) | copy-start | bytes 36868
  (8 other events, 8.5 us)
Sparse Core Ops, SparseCore 0:
  11.0 53.9 all-gather.7
  67.4 43.6 all-gather.5
  113.4 63.5 all-gather.9
  203.4 75.1 reduce-scatter.10
  282.9 69.8 reduce-scatter.8
  357.4 88.4 reduce-scatter.6
  450.6 88.1 reduce-scatter.4
  541.8 75.4 all-reduce.26
